TPU v7x, 32 devices: a whole 2x2x4 slice. The times are simulated.
32 devices in a mesh: dp: 4 (over y, core), tensor: 8 (over z, x).
Axes of the slice: x: 2, y: 2, z: 4, core: 2. Of those that a mesh axis runs over, the one named last changes fastest.
Arguments:
- patches: bfloat16 [32, 256, 1152], P('dp'), may hold values from -6 to 6
- conditioning: bfloat16 [32, 1152], P('dp'), may hold values from -6 to 6
- keep_count: int32 [32], P('dp'), may hold values from 64 to 192, as said below
- keep_index: int32 [32, 192], P('dp'), may hold values from 0 to 255, as said below
- mod_weight: bfloat16 [1152, 6912], P(None, 'tensor'), may hold values from -0.1875 to 0.1875
- mod_bias: bfloat16 [6912], P('tensor'), may hold values from -3 to 3
- qkv_weight: bfloat16 [3, 1152, 1152], P(None, None, 'tensor'), may hold values from -0.1875 to 0.1875
- qv_bias: bfloat16 [2, 1152], P(None, 'tensor'), may hold values from -3 to 3
- out_weight: bfloat16 [1152, 1152], P('tensor'), may hold values from -1.25 to 1.25
- out_bias: bfloat16 [1152], replicated, may hold values from -2 to 2
- up_weight: bfloat16 [1152, 4608], P(None, 'tensor'), may hold values from -0.1875 to 0.1875
- up_bias: bfloat16 [4608], P('tensor'), may hold values from -3 to 3
- down_weight: bfloat16 [4608, 1152], P('tensor'), may hold values from -0.09375 to 0.09375
- down_bias: bfloat16 [1152], replicated, may hold values from -2 to 2
- out_cotangent: bfloat16 [32, 192, 1152], P('dp'), may hold values from -6 to 6
Outputs:
- block_out: bfloat16 [32, 192, 1152], P('dp')
- grad_patches: bfloat16 [32, 256, 1152], P('dp')
- grad_conditioning: bfloat16 [32, 1152], P('dp')
- mod_weight_grad: float32 [1152, 6912], P(None, 'tensor')
- mod_bias_grad: float32 [6912], P('tensor')
- qkv_weight_grad: float32 [3, 1152, 1152], P(None, None, 'tensor')
- qv_bias_grad: float32 [2, 1152], P(None, 'tensor')
- out_weight_grad: float32 [1152, 1152], P('tensor')
- out_bias_grad: float32 [1152], replicated
- up_weight_grad: float32 [1152, 4608], P(None, 'tensor')
- up_bias_grad: float32 [4608], P('tensor')
- down_weight_grad: float32 [4608, 1152], P('tensor')
- down_bias_grad: float32 [1152], replicated
Inputs may be any that keep to these rules, and one draw needn't show every extreme that they name: `keep_count`: some image keeps 192 tokens and some keeps 64. A row of keep_index lists 192 different patch positions; the first keep_count of them are the image's kept tokens, the others are not read.
All inputs are finite; a program needn't handle non-finite values.
Results may differ from a plain program's by a relative error of at most 0.014.
The roundings to bfloat16 on the way count: a program that leaves them out, or rounds other values in their place, can miss the bound.
Values may be sent and summed in bfloat16 or wider, within the bound.
A program may use at most 192 MiB of HBM per device.

v0:
```python
import jax
import jax.numpy as jnp
from jax import lax
from jax.sharding import PartitionSpec as P

HD = 72


def layer_norm(inputs):
    centred = inputs - jnp.mean(inputs, axis=-1, keepdims=True)
    return centred * lax.rsqrt(jnp.mean(centred * centred, axis=-1, keepdims=True) + 1e-06)


def on_device(
    patches,
    conditioning,
    keep_count,
    keep_index,
    mod_weight,
    mod_bias,
    qkv_weight,
    qv_bias,
    out_weight,
    out_bias,
    up_weight,
    up_bias,
    down_weight,
    down_bias,
    out_cotangent,
):
    images, kept_rows = keep_index.shape
    model_width = patches.shape[2]
    local_width = qkv_weight.shape[2]
    local_heads = local_width // HD
    count_rows = images * kept_rows
    share_rows = kept_rows // lax.axis_size("tensor")
    share_start = lax.axis_index("tensor") * share_rows
    score_scale = HD ** (-0.5)
    live_rows = (jnp.arange(kept_rows, dtype=jnp.int32)[None, :] < keep_count[:, None]).astype(
        jnp.float32
    )[:, :, None]
    tokens = (
        jnp.take_along_axis(patches, keep_index[:, :, None], axis=1).astype(jnp.float32) * live_rows
    )
    cond_float = conditioning.astype(jnp.float32)
    silu_low = jax.nn.silu(cond_float).astype(jnp.bfloat16)
    mod_local = (
        jnp.dot(silu_low, mod_weight, preferred_element_type=jnp.float32)
        + mod_bias.astype(jnp.float32)
    ).astype(jnp.bfloat16)
    mod_full = lax.all_gather(mod_local, "tensor", axis=1, tiled=True).astype(jnp.float32)
    blocks = [
        mod_full[:, None, member * model_width : (member + 1) * model_width] for member in range(6)
    ]
    shift_one, scale_one, gate_one, shift_two, scale_two, gate_two = blocks
    norm_one = layer_norm(tokens)
    normed_one = (
        (norm_one * (1.0 + scale_one) + shift_one)
        .astype(jnp.bfloat16)
        .reshape(count_rows, model_width)
    )
    projected = jnp.einsum(
        "rd,tdh->trh", normed_one, qkv_weight, preferred_element_type=jnp.float32
    )
    bias_rows = jnp.stack([qv_bias[0], jnp.zeros_like(qv_bias[0]), qv_bias[1]]).astype(jnp.float32)[
        :, None, :
    ]
    qkv_rows = (projected + bias_rows).astype(jnp.bfloat16)
    queries, key_rows, value_rows = [
        qkv_rows[member].reshape(images, kept_rows, local_heads, HD) for member in range(3)
    ]
    key_live = live_rows[:, :, 0][:, None, None, :] > 0
    scores = (
        jnp.einsum("bqhd,bkhd->bhqk", queries, key_rows, preferred_element_type=jnp.float32)
        * score_scale
    )
    scores = jnp.where(key_live, scores, -1e30)
    row_top = jnp.max(scores, axis=-1, keepdims=True)
    exp_scores = jnp.exp(scores - row_top)
    row_total = jnp.sum(exp_scores, axis=-1, keepdims=True)
    log_total = row_top + jnp.log(row_total)
    weights_low = (exp_scores / row_total).astype(jnp.bfloat16)
    attended = jnp.einsum(
        "bhqk,bkhd->bqhd", weights_low, value_rows, preferred_element_type=jnp.float32
    )
    attended = attended.astype(jnp.bfloat16).reshape(count_rows, local_width)
    branch_part = jnp.dot(attended, out_weight, preferred_element_type=jnp.float32).reshape(
        images, kept_rows, model_width
    )
    out_bias_float = out_bias.astype(jnp.float32)
    branch = lax.psum(branch_part, "tensor") + out_bias_float
    middle = tokens + gate_one * branch
    norm_two = layer_norm(middle)
    normed_two = (norm_two * (1.0 + scale_two) + shift_two).astype(jnp.bfloat16)
    branch_share = lax.dynamic_slice_in_dim(branch, share_start, share_rows, 1)
    normed_rows = normed_two.reshape(count_rows, model_width)
    pre_act = jnp.dot(normed_rows, up_weight, preferred_element_type=jnp.float32) + up_bias.astype(
        jnp.float32
    )
    hidden = jax.nn.gelu(pre_act, approximate=True).astype(jnp.bfloat16)
    mlp_part = jnp.dot(hidden, down_weight, preferred_element_type=jnp.float32).reshape(
        images, kept_rows, model_width
    )
    down_bias_float = down_bias.astype(jnp.float32)
    mlp_out = (
        lax.psum(mlp_part.astype(jnp.bfloat16), "tensor").astype(jnp.float32) + down_bias_float
    )
    block_out = ((middle + gate_two * mlp_out) * live_rows).astype(jnp.bfloat16)
    mlp_share = lax.dynamic_slice_in_dim(mlp_out, share_start, share_rows, 1)
    grad_out = out_cotangent.astype(jnp.float32) * live_rows
    grad_share = lax.dynamic_slice_in_dim(grad_out, share_start, share_rows, 1)
    grad_gate_two = jnp.sum(grad_share * mlp_share, axis=1)
    grad_mlp = (gate_two * grad_out).astype(jnp.bfloat16).reshape(count_rows, model_width)
    down_bias_grad = jnp.sum(grad_mlp.astype(jnp.float32), axis=0)
    down_weight_grad = jnp.einsum("rf,rd->fd", hidden, grad_mlp, preferred_element_type=jnp.float32)
    grad_hidden = jnp.einsum("rd,fd->rf", grad_mlp, down_weight, preferred_element_type=jnp.float32)
    gelu_pull = jax.vjp(lambda inputs: jax.nn.gelu(inputs, approximate=True), pre_act)[1]
    grad_pre = gelu_pull(grad_hidden)[0].astype(jnp.bfloat16)
    up_bias_grad = jnp.sum(grad_pre.astype(jnp.float32), axis=0)
    up_weight_grad = jnp.einsum(
        "rd,rf->df", normed_rows, grad_pre, preferred_element_type=jnp.float32
    )
    grad_normed_two = jnp.einsum(
        "rf,df->rd", grad_pre, up_weight, preferred_element_type=jnp.float32
    ).reshape(images, kept_rows, model_width)
    grad_shift_two = jnp.sum(grad_normed_two, axis=1)
    grad_scale_two = jnp.sum(grad_normed_two * norm_two, axis=1)
    second_pull = jax.vjp(layer_norm, middle)[1]
    second_term = second_pull(grad_normed_two * (1.0 + scale_two))[0]
    grad_middle = grad_out + lax.psum(second_term, "tensor")
    grad_mid_share = lax.dynamic_slice_in_dim(grad_middle, share_start, share_rows, 1)
    grad_branch = (gate_one * grad_middle).astype(jnp.bfloat16)
    grad_gate_one = jnp.sum(grad_mid_share * branch_share, axis=1)
    grad_branch = grad_branch.reshape(count_rows, model_width)
    out_bias_grad = jnp.sum(grad_branch.astype(jnp.float32), axis=0)
    out_weight_grad = jnp.einsum(
        "rh,rd->hd", attended, grad_branch, preferred_element_type=jnp.float32
    )
    grad_att = jnp.einsum("rd,hd->rh", grad_branch, out_weight, preferred_element_type=jnp.float32)
    grad_att = grad_att.astype(jnp.bfloat16).reshape(images, kept_rows, local_heads, HD)
    scores_again = (
        jnp.einsum("bqhd,bkhd->bhqk", queries, key_rows, preferred_element_type=jnp.float32)
        * score_scale
    )
    weights_again = jnp.where(key_live, jnp.exp(scores_again - log_total), 0.0)
    grad_weights = jnp.einsum(
        "bqhd,bkhd->bhqk", grad_att, value_rows, preferred_element_type=jnp.float32
    )
    row_inner = jnp.sum(weights_again * grad_weights, axis=-1, keepdims=True)
    grad_scores = (weights_again * (grad_weights - row_inner)).astype(jnp.bfloat16)
    grad_values = jnp.einsum(
        "bhqk,bqhd->bkhd",
        weights_again.astype(jnp.bfloat16),
        grad_att,
        preferred_element_type=jnp.float32,
    )
    grad_queries = (
        jnp.einsum("bhqk,bkhd->bqhd", grad_scores, key_rows, preferred_element_type=jnp.float32)
        * score_scale
    )
    grad_keys = (
        jnp.einsum("bhqk,bqhd->bkhd", grad_scores, queries, preferred_element_type=jnp.float32)
        * score_scale
    )
    grad_qkv = jnp.stack(
        [
            member.reshape(count_rows, local_width)
            for member in (grad_queries, grad_keys, grad_values)
        ]
    ).astype(jnp.bfloat16)
    qkv_weight_grad = jnp.einsum(
        "rd,trh->tdh", normed_one, grad_qkv, preferred_element_type=jnp.float32
    )
    qv_bias_grad = jnp.stack(
        [
            jnp.sum(grad_qkv[0].astype(jnp.float32), axis=0),
            jnp.sum(grad_qkv[2].astype(jnp.float32), axis=0),
        ]
    )
    grad_normed_one = jnp.einsum(
        "trh,tdh->rd", grad_qkv, qkv_weight, preferred_element_type=jnp.float32
    ).reshape(images, kept_rows, model_width)
    grad_shift_one = jnp.sum(grad_normed_one, axis=1)
    grad_scale_one = jnp.sum(grad_normed_one * norm_one, axis=1)
    first_pull = jax.vjp(layer_norm, tokens)[1]
    first_term = first_pull(grad_normed_one * (1.0 + scale_one))[0]
    grad_tokens = (grad_middle + lax.psum(first_term, "tensor")) * live_rows
    grad_token_low = grad_tokens.astype(jnp.bfloat16)
    empty_grads = jnp.zeros(patches.shape, jnp.bfloat16)
    grad_patches = jax.vmap(
        lambda row_block, index_row, grad_block: row_block.at[index_row].set(grad_block)
    )(empty_grads, keep_index, grad_token_low)
    grad_mod_part = jnp.concatenate(
        [
            grad_shift_one,
            grad_scale_one,
            grad_gate_one,
            grad_shift_two,
            grad_scale_two,
            grad_gate_two,
        ],
        axis=1,
    )
    grad_mod = lax.psum_scatter(grad_mod_part, "tensor", scatter_dimension=1, tiled=True)
    silu_float = silu_low.astype(jnp.float32)
    mod_weight_grad = jnp.einsum("bd,bm->dm", silu_float, grad_mod, precision=lax.Precision.HIGHEST)
    mod_bias_grad = jnp.sum(grad_mod, axis=0)
    silu_term = jnp.einsum(
        "bm,dm->bd", grad_mod, mod_weight.astype(jnp.float32), precision=lax.Precision.HIGHEST
    )
    grad_silu = lax.psum(silu_term, "tensor")
    silu_pull = jax.vjp(jax.nn.silu, cond_float)[1]
    grad_conditioning = silu_pull(grad_silu)[0].astype(jnp.bfloat16)
    summed = (
        lax.psum(mod_weight_grad.astype(jnp.bfloat16), "dp").astype(jnp.float32),
        lax.psum(mod_bias_grad.astype(jnp.bfloat16), "dp").astype(jnp.float32),
        lax.psum(qkv_weight_grad.astype(jnp.bfloat16), "dp").astype(jnp.float32),
        lax.psum(qv_bias_grad.astype(jnp.bfloat16), "dp").astype(jnp.float32),
        lax.psum(out_weight_grad.astype(jnp.bfloat16), "dp").astype(jnp.float32),
        lax.psum(out_bias_grad.astype(jnp.bfloat16), "dp").astype(jnp.float32),
        lax.psum(up_weight_grad.astype(jnp.bfloat16), "dp").astype(jnp.float32),
        lax.psum(up_bias_grad.astype(jnp.bfloat16), "dp").astype(jnp.float32),
        lax.psum(down_weight_grad.astype(jnp.bfloat16), "dp").astype(jnp.float32),
        lax.psum(down_bias_grad.astype(jnp.bfloat16), "dp").astype(jnp.float32),
    )
    return (block_out, grad_patches, grad_conditioning) + tuple(summed)


def solution(mesh):
    placed = (
        P("dp", None, None),
        P("dp", None),
        P("dp"),
        P("dp", None),
        P(None, "tensor"),
        P("tensor"),
        P(None, None, "tensor"),
        P(None, "tensor"),
        P("tensor", None),
        P(),
        P(None, "tensor"),
        P("tensor"),
        P("tensor", None),
        P(),
        P("dp", None, None),
    )
    return jax.shard_map(
        on_device,
        mesh=mesh,
        in_specs=placed,
        out_specs=(
            P("dp", None, None),
            P("dp", None, None),
            P("dp", None),
            P(None, "tensor"),
            P("tensor"),
            P(None, None, "tensor"),
            P(None, "tensor"),
            P("tensor", None),
            P(),
            P(None, "tensor"),
            P("tensor"),
            P("tensor", None),
            P(),
        ),
        check_vma=False,
    )
```

profile of v0, /device:TPU:0, one launch (start us, length us, event | category | flops | bytes accessed | tf_op | source)
XLA Modules:
  0.0 1267.2 jit_solution(10761815162576918113)
XLA Ops:
  9.1 32.2 %gather_fusion = bf16[1536,1152]{1,0:T(8,128)(2,1)} fusion(bf16[8,256,1152]{2,1,0:T(8,128)(2,1)} %param.15, s32[1536]{0:T(1024)S(1)} %reshape.255), kind=kCustom, calls=%fused_computation | custom fusion | bytes 7090176 | tf_op jit(solution)/shard_map/jit(take_along_axis)/gather | solution.py:43
  48.2 32.4 %all-gather = bf16[8,864,8]{1,2,0:T(8,128)(2,1)S(1)} all-gather(bf16[1,864,8]{1,2,0:T(8,128)(2,1)S(1)} %fusion.46), channel_id=1, replica_groups=mesh['dp'=4,'tensor'=8] {'tensor'}, dimensions={0}, use_global_device_ids=true | all-gather | bytes 124416 | tf_op jit(solution)/shard_map/all_gather | solution.py:51
  109.8 222.4 %all-reduce.8.cloned.1.call-done = f32[8,192,1152]{2,1,0:T(8,128)} async-done(((f32[8,192,1152]{2,1,0:T(8,128)}), f32[8,192,1152]{2,1,0:T(8,128)}) %all-reduce.8.cloned.1.call-update) | async-done | bytes 7077904 | tf_op jit(solution)/shard_map/psum | solution.py:91
  332.2 6.9 fusion.85
  344.4 5.8 fusion.81
  355.7 5.1 fusion.92
  360.8 6.3 multiply_reduce_fusion.3
  367.2 5.4 multiply_reduce_fusion
  372.6 120.3 %all-reduce.10.cloned.1.call-done = bf16[8,192,1152]{2,1,0:T(8,128)(2,1)} async-done(((bf16[8,192,1152]{2,1,0:T(8,128)(2,1)}), bf16[8,192,1152]{2,1,0:T(8,128)(2,1)}) %all-reduce.10.cloned.1.call-update) | async-done | bytes 3538960 | tf_op jit(solution)/shard_map/psum | solution.py:106
  493.0 17.5 %broadcast_add_fusion = (f32[8,192,1152]{2,1,0:T(8,128)}, bf16[8,192,1152]{2,1,0:T(8,128)(2,1)}, f32[8,192,1152]{2,1,0:T(8,128)}, f32[8,192,1152]{2,1,0:T(8,128)}) fusion(f32[8,192]{1,0:T(8,128)S(1)} %negate_multiply_fusion.1, f32[8,192]{1,0:T(8,128)S(1)} %multiply_multiply_fusion.4, f32[8,192,1152]{2,1,0:T(8,128)} %copy-done.1, ...), kind=kLoop, calls=%fused_computation.41 | loop fusion | flops 26542080 | bytes 46115328 | tf_op jit(solution)/shard_map/transpose(jvp())/add_any | solution.py:10
  512.2 6.2 convolution_convert_fusion.2
  524.2 217.0 %all-reduce.12.cloned.1.call-done = f32[8,192,1152]{2,1,0:T(8,128)} async-done(((f32[8,192,1152]{2,1,0:T(8,128)}), f32[8,192,1152]{2,1,0:T(8,128)}) %all-reduce.12.cloned.1.call-update) | async-done | bytes 7077904 | tf_op jit(solution)/shard_map/psum | solution.py:130
  741.2 7.3 fusion.83
  771.3 8.2 multiply_reduce_fusion.2
  784.6 5.8 fusion.1
  791.1 9.1 multiply_reduce_fusion.1
  809.1 4.8 fusion.19
  813.9 73.5 %reduce-scatter.4.cloned.1.call-done = f32[864,8]{1,0:T(8,128)} async-done(((f32[6912,8]{1,0:T(8,128)}), f32[864,8]{1,0:T(8,128)}) %reduce-scatter.4.cloned.1.call-update) | async-done | bytes 27664
  892.8 11.2 all-reduce
  907.9 36.0 %psum.109 = f32[8,1152]{1,0:T(8,128)S(1)} all-reduce(f32[8,1152]{1,0:T(8,128)S(1)} %fusion.58), channel_id=1, replica_groups=mesh['dp'=4,'tensor'=8] {'tensor'}, use_global_device_ids=true, to_apply=%region_23.24 | all-reduce | flops 9216 | bytes 73728 | tf_op jit(solution)/shard_map/psum | solution.py:211
  944.6 61.4 %all-reduce.16.cloned.1.call-done = (bf16[1152,864]{0,1:T(8,128)(2,1)}, bf16[3,1152,144]{1,2,0:T(8,128)(2,1)}, bf16[144,1152]{1,0:T(8,128)(2,1)}, bf16[1152,576]{0,1:T(8,128)(2,1)}, bf16[576,1152]{1,0:T(8,128)(2,1)}) async-done(((bf16[1152,864]{0,1:T(8,128)(2,1)}, bf16[3,1152,144]{1,2,0:T(8,128)(2,1)}, bf16[144,1152]{1,0:T(8,128)(2,1)}, bf16[1152,576]{0,1:T(8,128)(2,1)}, bf16[576,1152]{1,0:T(8,128)(2,1)}), ...) | async-done | bytes 5971984 | tf_op jit(solution)/shard_map/psum | solution.py:215
  1016.6 224.6 %all-reduce.14.cloned.1.call-done = f32[8,192,1152]{2,1,0:T(8,128)} async-done(((f32[8,192,1152]{2,1,0:T(8,128)}), f32[8,192,1152]{2,1,0:T(8,128)}) %all-reduce.14.cloned.1.call-update) | async-done | bytes 7077904 | tf_op jit(solution)/shard_map/psum | solution.py:187
  1241.2 7.4 multiply_convert_fusion
  1248.7 11.3 scatter_custom_fusion
  (209 shorter events, 113.7 us)
Async XLA Ops:
  7.2 40.4 %copy-start = (bf16[1152,864]{0,1:T(8,128)(2,1)S(1)}, bf16[1152,864]{0,1:T(8,128)(2,1)}, u32[]{:S(2)}) copy-start(bf16[1152,864]{0,1:T(8,128)(2,1)} %param.19) | copy-start | bytes 5971972
  7.2 325.1 %all-reduce.8.cloned.1.call-start = ((), (), s32[]{:S(2)}) async-start(), calls=%async_computation.1 | async-start | bytes 14155776 | tf_op jit(solution)/shard_map/psum | solution.py:91
  8.9 85.2 %copy-start.28 = (pred[8,192]{1,0:T(8,128)(4,1)}, pred[8,192]{1,0:T(8,128)(4,1)S(1)}, u32[]{:S(2)}) copy-start(pred[8,192]{1,0:T(8,128)(4,1)S(1)} %get-tuple-element.56) | copy-start | bytes 4612
  9.0 71.9 %copy-start.27 = (pred[1536]{0:T(1024)(128)(4,1)}, pred[1536]{0:T(1024)(128)(4,1)S(1)}, u32[]{:S(2)}) copy-start(pred[1536]{0:T(1024)(128)(4,1)S(1)} %broadcast_in_dim.78) | copy-start | bytes 4612
  41.3 6.2 copy-start.34
  41.3 6.2 copy-start.35
  41.3 6.2 copy-start.24
  99.7 393.3 %all-reduce.10.cloned.1.call-start = ((), (), s32[]{:S(2)}) async-start(), calls=%async_computation.2 | async-start | bytes 7077888 | tf_op jit(solution)/shard_map/psum | solution.py:106
  100.4 5.2 copy-start.41
  343.6 6.6 copy-start.10
  344.4 5.8 copy-start.42
  350.2 4.8 copy-start.46
  355.1 386.1 %all-reduce.12.cloned.1.call-start = ((), (), s32[]{:S(2)}) async-start(), calls=%async_computation.3 | async-start | bytes 14155776 | tf_op jit(solution)/shard_map/psum | solution.py:130
  360.8 6.4 copy-start.3
  510.5 376.9 %reduce-scatter.4.cloned.1.call-start = ((), (), s32[]{:S(2)}) async-start(), calls=%async_computation.5 | async-start | bytes 3981312
  512.1 6.2 copy-start.9
  512.2 6.2 copy-start.47
  524.1 226.1 %copy-start.23 = (bf16[144,1152]{1,0:T(8,128)(2,1)S(1)}, bf16[144,1152]{1,0:T(8,128)(2,1)}, u32[]{:S(2)}) copy-start(bf16[144,1152]{1,0:T(8,128)(2,1)} %param.23) | copy-start | bytes 995332
  748.5 5.4 copy-start.29
  752.3 5.2 copy-start.17
  808.8 197.2 %all-reduce.16.cloned.1.call-start = ((), (), s32[]{:S(2)}) async-start(), calls=%async_computation.6 | async-start | bytes 11943936 | tf_op jit(solution)/shard_map/psum | solution.py:215
  891.4 349.8 %all-reduce.14.cloned.1.call-start = ((), (), s32[]{:S(2)}) async-start(), calls=%async_computation.4 | async-start | bytes 14155776 | tf_op jit(solution)/shard_map/psum | solution.py:187
  1006.0 5.8 copy-start.21
  1008.0 5.3 copy-start.19
  (30 other events, 57.6 us)
Sparse Core Ops, SparseCore 0:
  99.8 232.3 all-reduce.7
  355.2 137.7 all-reduce.9
  510.6 230.5 all-reduce.11
  808.9 78.4 reduce-scatter.3
  891.5 114.4 all-reduce.15
  1009.7 231.5 all-reduce.13
where the time goes:
time: 1280 us; the launch traced here: 1270 us
  waiting for transfers between devices  920 us (72%)
  other arithmetic  105 us (8%)
  blocking collectives  79.6 us (6%)
  local copies, waits for them, and re-layouts  74.9 us (6%)
  matrix products  71.1 us (6%)
  between operations  15.2 us (1%)
    psum x1, waiting for transfers between devices, on_device(): grad_tokens = (grad_middle + lax.psum(first_term, 'tensor')) * live_rows  225 us
    psum x1, waiting for transfers between devices, on_device(): branch = lax.psum(branch_part, 'tensor') + out_bias_float  222 us
    psum x1, waiting for transfers between devices, on_device(): grad_middle = grad_out + lax.psum(second_term, 'tensor')  217 us
    psum x1, waiting for transfers between devices, on_device(): lax.psum(mlp_part.astype(jnp.bfloat16), 'tensor').astype(jnp.float32)  120 us
    unnamed x7, waiting for transfers between devices  74 us
    psum x1, waiting for transfers between devices, on_device(): lax.psum(mod_weight_grad.astype(jnp.bfloat16), 'dp').astype(jnp.float32)  61.4 us
    psum x1, blocking collectives, on_device(): grad_silu = lax.psum(silu_term, 'tensor')  36 us
    all_gather x1, blocking collectives, on_device(): lax.all_gather(mod_local, 'tensor', axis=1, tiled=True).astype(jnp.float32)  32.4 us
  transfers between devices with their start and end apart: 6, of which 6 were waited for; matrix products, arithmetic and copies ran while one was open for 5% of the time, Pallas kernels for 0%

commit v1 on v0

--- a/solution.py
+++ b/solution.py
@@ -208,7 +208,11 @@
     silu_term = jnp.einsum(
         "bm,dm->bd", grad_mod, mod_weight.astype(jnp.float32), precision=lax.Precision.HIGHEST
     )
-    grad_silu = lax.psum(silu_term, "tensor")
+    grad_silu = silu_term
+    for hop in (1, 2, 4):
+        grad_silu = grad_silu + lax.ppermute(
+            grad_silu, "tensor", [(dev, dev ^ hop) for dev in range(8)]
+        )
     silu_pull = jax.vjp(jax.nn.silu, cond_float)[1]
     grad_conditioning = silu_pull(grad_silu)[0].astype(jnp.bfloat16)
     summed = (

time: 1280 us -> 1280 us (level)
  blocking collectives: 79.6 us -> 44.2 us
  waiting for transfers between devices: 920 us -> 950 us
    psum x1 -> x0, blocking collectives: 36 us -> none  [on_device(): grad_silu = lax.psum(silu_term, 'tensor')]
    psum x1, waiting for transfers between devices: 61.4 us -> 87.2 us  [on_device(): lax.psum(mod_weight_grad.astype(jnp.bfloat16), 'dp').astype(jnp.float32)]
  transfers between devices with their start and end apart: 6 -> 9, of which waited for: 6 -> 8; matrix products, arithmetic and copies ran while one was open for 5% -> 5% of each run, Pallas kernels for 0% -> 0%
where the time goes in v1:
time: 1280 us; the launch traced here: 1270 us
  waiting for transfers between devices  950 us (74%)
  other arithmetic  105 us (8%)
  local copies, waits for them, and re-layouts  75.1 us (6%)
  matrix products  71.1 us (6%)
  blocking collectives  44.2 us (3%)
  between operations  15.2 us (1%)
    psum x1, waiting for transfers between devices, on_device(): grad_tokens = (grad_middle + lax.psum(first_term, 'tensor')) * live_rows  225 us
    psum x1, waiting for transfers between devices, on_device(): branch = lax.psum(branch_part, 'tensor') + out_bias_float  222 us
    psum x1, waiting for transfers between devices, on_device(): grad_middle = grad_out + lax.psum(second_term, 'tensor')  217 us
    psum x1, waiting for transfers between devices, on_device(): lax.psum(mlp_part.astype(jnp.bfloat16), 'tensor').astype(jnp.float32)  120 us
    psum x1, waiting for transfers between devices, on_device(): lax.psum(mod_weight_grad.astype(jnp.bfloat16), 'dp').astype(jnp.float32)  87.2 us
    unnamed x7, waiting for transfers between devices  74 us
    all_gather x1, blocking collectives, on_device(): lax.all_gather(mod_local, 'tensor', axis=1, tiled=True).astype(jnp.float32)  32.4 us
    gather x3, local copies, waits for them, and re-layouts, on_device(): jnp.take_along_axis(patches, keep_index[:, :, None], axis=1)  32.3 us
  transfers between devices with their start and end apart: 9, of which 8 were waited for; matrix products, arithmetic and copies ran while one was open for 5% of the time, Pallas kernels for 0%

profile of v1, /device:TPU:0, one launch (start us, length us, event | category | flops | bytes accessed | tf_op | source)
XLA Modules:
  0.0 1267.4 jit_solution(10082893632976355354)
XLA Ops:
  9.1 32.2 %gather_fusion = bf16[1536,1152]{1,0:T(8,128)(2,1)} fusion(bf16[8,256,1152]{2,1,0:T(8,128)(2,1)} %param.15, s32[1536]{0:T(1024)S(1)} %reshape.255), kind=kCustom, calls=%fused_computation | custom fusion | bytes 7090176 | tf_op jit(solution)/shard_map/jit(take_along_axis)/gather | solution.py:43
  48.2 32.4 %all-gather = bf16[8,864,8]{1,2,0:T(8,128)(2,1)S(1)} all-gather(bf16[1,864,8]{1,2,0:T(8,128)(2,1)S(1)} %fusion.46), channel_id=1, replica_groups=mesh['dp'=4,'tensor'=8] {'tensor'}, dimensions={0}, use_global_device_ids=true | all-gather | bytes 124416 | tf_op jit(solution)/shard_map/all_gather | solution.py:51
  109.8 222.4 %all-reduce.8.cloned.1.call-done = f32[8,192,1152]{2,1,0:T(8,128)} async-done(((f32[8,192,1152]{2,1,0:T(8,128)}), f32[8,192,1152]{2,1,0:T(8,128)}) %all-reduce.8.cloned.1.call-update) | async-done | bytes 7077904 | tf_op jit(solution)/shard_map/psum | solution.py:91
  332.2 6.9 fusion.85
  344.4 5.8 fusion.81
  350.2 4.8 convolution_convert_fusion
  355.7 5.1 fusion.92
  360.8 6.3 multiply_reduce_fusion.3
  367.2 5.4 multiply_reduce_fusion
  372.6 120.3 %all-reduce.10.cloned.1.call-done = bf16[8,192,1152]{2,1,0:T(8,128)(2,1)} async-done(((bf16[8,192,1152]{2,1,0:T(8,128)(2,1)}), bf16[8,192,1152]{2,1,0:T(8,128)(2,1)}) %all-reduce.10.cloned.1.call-update) | async-done | bytes 3538960 | tf_op jit(solution)/shard_map/psum | solution.py:106
  493.0 17.5 %broadcast_add_fusion = (f32[8,192,1152]{2,1,0:T(8,128)}, bf16[8,192,1152]{2,1,0:T(8,128)(2,1)}, f32[8,192,1152]{2,1,0:T(8,128)}, f32[8,192,1152]{2,1,0:T(8,128)}) fusion(f32[8,192]{1,0:T(8,128)S(1)} %negate_multiply_fusion.1, f32[8,192]{1,0:T(8,128)S(1)} %multiply_multiply_fusion.4, f32[8,192,1152]{2,1,0:T(8,128)} %copy-done.1, ...), kind=kLoop, calls=%fused_computation.41 | loop fusion | flops 26542080 | bytes 46115328 | tf_op jit(solution)/shard_map/transpose(jvp())/add_any | solution.py:10
  512.2 6.2 convolution_convert_fusion.2
  524.2 217.0 %all-reduce.12.cloned.1.call-done = f32[8,192,1152]{2,1,0:T(8,128)} async-done(((f32[8,192,1152]{2,1,0:T(8,128)}), f32[8,192,1152]{2,1,0:T(8,128)}) %all-reduce.12.cloned.1.call-update) | async-done | bytes 7077904 | tf_op jit(solution)/shard_map/psum | solution.py:130
  741.2 7.3 fusion.83
  771.3 8.2 multiply_reduce_fusion.2
  784.6 5.8 fusion.1
  791.1 9.1 multiply_reduce_fusion.1
  809.1 4.8 fusion.19
  813.9 73.5 %reduce-scatter.4.cloned.1.call-done = f32[864,8]{1,0:T(8,128)} async-done(((f32[6912,8]{1,0:T(8,128)}), f32[864,8]{1,0:T(8,128)}) %reduce-scatter.4.cloned.1.call-update) | async-done | bytes 27664
  903.5 11.8 all-reduce
  918.9 87.2 %all-reduce.16.cloned.1.call-done = (bf16[1152,864]{0,1:T(8,128)(2,1)}, bf16[3,1152,144]{1,2,0:T(8,128)(2,1)}, bf16[144,1152]{1,0:T(8,128)(2,1)}, bf16[1152,576]{0,1:T(8,128)(2,1)}, bf16[576,1152]{1,0:T(8,128)(2,1)}) async-done(((bf16[1152,864]{0,1:T(8,128)(2,1)}, bf16[3,1152,144]{1,2,0:T(8,128)(2,1)}, bf16[144,1152]{1,0:T(8,128)(2,1)}, bf16[1152,576]{0,1:T(8,128)(2,1)}, bf16[576,1152]{1,0:T(8,128)(2,1)}), ...) | async-done | bytes 5971984 | tf_op jit(solution)/shard_map/psum | solution.py:219
  1016.8 224.6 %all-reduce.14.cloned.1.call-done = f32[8,192,1152]{2,1,0:T(8,128)} async-done(((f32[8,192,1152]{2,1,0:T(8,128)}), f32[8,192,1152]{2,1,0:T(8,128)}) %all-reduce.14.cloned.1.call-update) | async-done | bytes 7077904 | tf_op jit(solution)/shard_map/psum | solution.py:187
  1241.4 7.4 multiply_convert_fusion
  1248.8 11.3 scatter_custom_fusion
  (216 shorter events, 118.6 us)
Async XLA Ops:
  7.2 40.4 %copy-start = (bf16[1152,864]{0,1:T(8,128)(2,1)S(1)}, bf16[1152,864]{0,1:T(8,128)(2,1)}, u32[]{:S(2)}) copy-start(bf16[1152,864]{0,1:T(8,128)(2,1)} %param.19) | copy-start | bytes 5971972
  7.2 325.1 %all-reduce.8.cloned.1.call-start = ((), (), s32[]{:S(2)}) async-start(), calls=%async_computation.1 | async-start | bytes 14155776 | tf_op jit(solution)/shard_map/psum | solution.py:91
  8.9 85.2 %copy-start.28 = (pred[8,192]{1,0:T(8,128)(4,1)}, pred[8,192]{1,0:T(8,128)(4,1)S(1)}, u32[]{:S(2)}) copy-start(pred[8,192]{1,0:T(8,128)(4,1)S(1)} %get-tuple-element.56) | copy-start | bytes 4612
  9.0 71.9 %copy-start.27 = (pred[1536]{0:T(1024)(128)(4,1)}, pred[1536]{0:T(1024)(128)(4,1)S(1)}, u32[]{:S(2)}) copy-start(pred[1536]{0:T(1024)(128)(4,1)S(1)} %broadcast_in_dim.78) | copy-start | bytes 4612
  41.3 6.2 copy-start.34
  41.3 6.2 copy-start.35
  41.3 6.2 copy-start.24
  99.7 393.3 %all-reduce.10.cloned.1.call-start = ((), (), s32[]{:S(2)}) async-start(), calls=%async_computation.2 | async-start | bytes 7077888 | tf_op jit(solution)/shard_map/psum | solution.py:106
  343.6 6.6 copy-start.10
  344.4 5.8 copy-start.42
  355.1 386.1 %all-reduce.12.cloned.1.call-start = ((), (), s32[]{:S(2)}) async-start(), calls=%async_computation.3 | async-start | bytes 14155776 | tf_op jit(solution)/shard_map/psum | solution.py:130
  360.8 6.4 copy-start.3
  510.5 376.9 %reduce-scatter.4.cloned.1.call-start = ((), (), s32[]{:S(2)}) async-start(), calls=%async_computation.5 | async-start | bytes 3981312
  512.1 6.2 copy-start.9
  512.2 6.2 copy-start.47
  524.1 226.1 %copy-start.23 = (bf16[144,1152]{1,0:T(8,128)(2,1)S(1)}, bf16[144,1152]{1,0:T(8,128)(2,1)}, u32[]{:S(2)}) copy-start(bf16[144,1152]{1,0:T(8,128)(2,1)} %param.23) | copy-start | bytes 995332
  808.8 197.4 %all-reduce.16.cloned.1.call-start = ((), (), s32[]{:S(2)}) async-start(), calls=%async_computation.6 | async-start | bytes 11943936 | tf_op jit(solution)/shard_map/psum | solution.py:219
  891.4 350.0 %all-reduce.14.cloned.1.call-start = ((), (), s32[]{:S(2)}) async-start(), calls=%async_computation.4 | async-start | bytes 14155776 | tf_op jit(solution)/shard_map/psum | solution.py:187
  891.5 12.0 copy-start.30
  891.5 12.0 copy-start.31
  891.5 12.0 copy-start.37
  893.5 4.0 collective-permute-start
  897.5 4.0 collective-permute-start.1
  901.5 16.8 %collective-permute-start.2 = (f32[8,1152]{1,0:T(8,128)S(1)}, f32[8,1152]{1,0:T(8,128)S(1)}, u32[]{:S(2)}, u32[]{:S(2)}) collective-permute-start(f32[8,1152]{1,0:T(8,128)S(1)} %add.220), channel_id=1, source_target_pairs={{0,4},{1,5},{2,6},{3,7},{4,0},{5,1},{6,2},{7,3},{8,12},{9,13},{10,... | collective-permute-start | bytes 110600 | tf_op jit(solution)/shard_map/ppermute | solution.py:213
  (33 other events, 90.5 us)
Sparse Core Ops, SparseCore 0:
  99.8 232.3 all-reduce.7
  355.2 137.7 all-reduce.9
  510.6 230.5 all-reduce.11
  808.9 78.4 reduce-scatter.3
  891.5 114.5 all-reduce.15
  1009.8 231.5 all-reduce.13
